TPU v7x, 512 devices: a whole 4x4x16 slice. The times are simulated.
512 devices in a mesh: span: 64 (over z_lo, x, core), chord: 8 (over z_hi, y).
Axes of the slice: x: 4, y: 4, z: 16 (z_hi: 2, z_lo: 8; z = z_hi * 8 + z_lo), core: 2. Of those that a mesh axis runs over, the one named last changes fastest.
Arguments:
- adjoint_flow: float32 [5, 16, 512, 1024], P(None, None, 'span', 'chord'), may hold values from -6 to 6
- flow_grad: float32 [5, 16, 512, 1024], P(None, None, 'span', 'chord'), may hold values from -6 to 6
- diagonal: float32 [16, 512, 1024], P(None, 'span', 'chord'), may hold values from 4 to 6
- couplings: float32 [3, 16, 512, 1024], P(None, None, 'span', 'chord'), may hold values from 0.3 to 1.5
- upwind: float32 [3, 5, 5], replicated, may hold values from -2.5 to 2.5
- downwind: float32 [3, 5, 5], replicated, may hold values from -2.5 to 2.5
- pressure_row: float32 [5], replicated, may hold values from -4 to 4
- face_normal: float32 [3, 512, 1024], P(None, 'span', 'chord'), may hold values from -6 to 6
- face_node: int32 [512, 1024], P('span', 'chord'), may hold values from 0 to 65535, as said below
- face_count: int32 [64, 8], P('span', 'chord'), may hold values from 128 to 1024, as said below
- adjoint_shell: float32 [6, 65536], P(None, 'span'), may hold values from -6 to 6
- shell_grad: float32 [6, 65536], P(None, 'span'), may hold values from -6 to 6
- node_precond: float32 [6, 6, 65536], P(None, None, 'span'), as said below
- element_stiffness: float32 [24, 24, 65536], P(None, None, ('span', 'chord')), as said below
- connectivity: int32 [4, 65536], P(None, ('span', 'chord')), may hold values from 0 to 65535, as said below
Outputs:
- flow_adjoint: float32 [5, 16, 512, 1024], P(None, None, 'span', 'chord')
- shell_adjoint: float32 [6, 65536], P(None, 'span')
Inputs may be any that keep to these rules, and one draw needn't show every extreme that they name: `face_node`: a wall face in the span cells of span index s names a node from max(s - 1, 0) * 1024 to min(s + 2, 64) * 1024 - 1. `face_count`: on each device the wall faces in use are the first ones in span-major, chord-minor order. `connectivity`: the elements of span index s use nodes from s * 1024 to min((s + 1) * 1024 + 64, 65536) - 1. `node_precond`: each node block is near 0.15 times the identity. `element_stiffness`: each element block is symmetric and near the identity.
All inputs are finite; a program needn't handle non-finite values.
Results may differ from a plain program's by a relative error of at most 0.00013.
Values sent between devices are 32-bit elements; how exact they have to be, the bound alone decides.
No kernel may reach another device: no remote copies, remote signals or barrier semaphores. Data moves between devices by JAX's collectives and lax.ppermute only.
A program may use at most 64 MiB of HBM per device.

v0:
```python
import jax
import jax.numpy as jnp
from jax import lax
from jax.sharding import PartitionSpec as P

NB = 64
SW = 4
SS = 3


def shifted(value, axis, steps):
    count = lax.axis_size(axis)
    initial, last = (max(0, -steps), min(count, count - steps))
    return lax.ppermute(value, axis, [(source, source + steps) for source in range(initial, last)])


def with_halo(cells, sides, width):
    for axis, dim in sides:
        count = lax.axis_size(axis)
        ends = count - 1
        head = lax.slice_in_dim(cells, 0, width, axis=dim)
        tail = lax.slice_in_dim(cells, cells.shape[dim] - width, cells.shape[dim], axis=dim)
        cells = jnp.concatenate(
            [
                lax.ppermute(tail, axis, [(i, (i + 1) % count) for i in range(ends)]),
                cells,
                lax.ppermute(head, axis, [((i + 1) % count, i) for i in range(ends)]),
            ],
            axis=dim,
        )
    return cells


def relax_cells(state, inv_diag, couplings, source, upwind, downwind):
    centre = state[:, :, 1:-1, 1:-1]
    normal_pad = jnp.pad(centre, ((0, 0), (1, 1), (0, 0), (0, 0)))
    pairs = (
        (normal_pad[:, 2:], normal_pad[:, :-2]),
        (state[:, :, 2:, 1:-1], state[:, :, :-2, 1:-1]),
        (state[:, :, 1:-1, 2:], state[:, :, 1:-1, :-2]),
    )
    neighbours = jnp.zeros_like(source)
    for direction in range(3):
        forward, backward = pairs[direction]
        flux_term = jnp.einsum(
            "ij,jnsc->insc", upwind[direction], forward, precision=lax.Precision.HIGHEST
        )
        flux_term = flux_term + jnp.einsum(
            "ij,jnsc->insc", downwind[direction], backward, precision=lax.Precision.HIGHEST
        )
        neighbours = neighbours + couplings[direction][None] * flux_term
    return inv_diag[None] * (source + neighbours)


def spread(partial_value, node_dev):
    own_block = partial_value[:, node_dev : 2 * node_dev]
    from_lower = shifted(partial_value[:, 2 * node_dev :], "span", 1)
    from_upper = shifted(partial_value[:, :node_dev], "span", -1)
    return own_block + from_lower + from_upper


def element_terms(field, element_stiffness, local_nodes):
    node_dev = field.shape[1]
    count_elems = local_nodes.shape[1]
    rim_nodes = shifted(field[:, :NB], "span", -1)
    extended = jnp.concatenate([field, rim_nodes], axis=1)
    element_values = extended[:, local_nodes]
    element_values = jnp.transpose(element_values, (1, 0, 2)).reshape(24, count_elems)
    element_forces = jnp.einsum(
        "ije,je->ie", element_stiffness, element_values, precision=lax.Precision.HIGHEST
    )
    element_forces = jnp.transpose(element_forces.reshape(4, 6, count_elems), (1, 0, 2)).reshape(
        6, 4 * count_elems
    )
    assembled = jax.ops.segment_sum(element_forces.T, local_nodes.reshape(-1), node_dev + NB).T
    spill = shifted(assembled[:, node_dev:], "span", 1)
    return assembled[:, :node_dev].at[:, :NB].add(spill)


def per_device(
    adjoint_flow,
    flow_grad,
    diagonal,
    couplings,
    upwind,
    downwind,
    pressure_row,
    face_normal,
    face_node,
    face_count,
    adjoint_shell,
    shell_grad,
    node_precond,
    element_stiffness,
    connectivity,
):
    span_at = lax.axis_index("span")
    node_dev = adjoint_shell.shape[1]
    wall_layer = adjoint_flow[:, 0]
    span_cells = wall_layer.shape[1]
    chord_cells = wall_layer.shape[2]
    local_index = (
        jnp.arange(span_cells, dtype=jnp.int32)[:, None] * chord_cells
        + jnp.arange(chord_cells, dtype=jnp.int32)[None, :]
    )
    active = (local_index < face_count[0, 0]).astype(jnp.float32)
    pressure = (
        jnp.einsum("j,jsc->sc", pressure_row, wall_layer, precision=lax.Precision.HIGHEST) * active
    )
    loads_face = face_normal * pressure[None]
    reach_index = face_node - (span_at - 1) * node_dev
    partial_value = jax.ops.segment_sum(
        loads_face.reshape(3, -1).T, reach_index.reshape(-1), 3 * node_dev
    ).T
    partial_value = lax.psum(partial_value, "chord")
    node_load = spread(partial_value, node_dev)
    load_full = jnp.concatenate([node_load, jnp.zeros((3, node_dev), jnp.float32)], axis=0)
    local_nodes = connectivity - span_at * node_dev
    shell_state = adjoint_shell
    for turn_index in range(SS):
        local_forces = element_terms(shell_state, element_stiffness, local_nodes)
        stiff_total = lax.psum(local_forces, "chord")
        residual = shell_grad - load_full - stiff_total
        shell_state = shell_state + jnp.einsum(
            "ijn,jn->in", node_precond, residual, precision=lax.Precision.HIGHEST
        )
    reach = with_halo(shell_state[:3], (("span", 1),), node_dev)
    picked = reach[:, reach_index]
    disp = jnp.einsum("isc,isc->sc", face_normal, picked, precision=lax.Precision.HIGHEST) * active
    source = flow_grad.at[:, 0].add(-pressure_row[:, None, None] * disp[None])
    inv_diag = 1.0 / diagonal
    state = adjoint_flow
    for turn_index in range(SW):
        padded = with_halo(state, (("span", 2), ("chord", 3)), 1)
        state = relax_cells(padded, inv_diag, couplings, source, upwind, downwind)
    return (state, shell_state)


def solution(mesh):
    return jax.shard_map(
        per_device,
        mesh=mesh,
        in_specs=(
            P(None, None, "span", "chord"),
            P(None, None, "span", "chord"),
            P(None, "span", "chord"),
            P(None, None, "span", "chord"),
            P(),
            P(),
            P(),
            P(None, "span", "chord"),
            P("span", "chord"),
            P("span", "chord"),
            P(None, "span"),
            P(None, "span"),
            P(None, None, "span"),
            P(None, None, ("span", "chord")),
            P(None, ("span", "chord")),
        ),
        out_specs=(P(None, None, "span", "chord"), P(None, "span")),
        check_vma=False,
    )
```

profile of v0, /device:TPU:223, one launch (start us, length us, event | category | flops | bytes accessed | tf_op | source)
XLA Modules:
  0.0 633.0 jit_solution(17247283147842668898)
XLA Ops:
  5.8 5.1 collective-permute-start.11
  22.8 5.7 collective-permute-start.3
  28.8 6.4 %scatter_custom_fusion = f32[3072,3]{1,0:T(8,128)S(1)} fusion(s32[1024]{0:T(1024)S(1)} %subtract_bitcast_fusion.3, f32[1024,3]{1,0:T(8,128)S(1)} %bitcast.192, f32[]{:T(128)} %constant.114.clone.1), kind=kCustom, calls=%fused_computation.52 | custom fusion | flops 3072 | bytes 36868 | tf_op jit(solution)/shard_map/scatter-add | solution.py:112
  36.7 194.2 %all-reduce.5 = (f32[6,1024]{0,1:T(8,128)}, f32[3,3072]{0,1:T(8,128)}) all-reduce(f32[6,1024]{0,1:T(8,128)S(1)} %fusion.84, f32[3,3072]{0,1:T(8,128)S(1)} %bitcast.181), channel_id=1, replica_groups=mesh['span'=64,'chord'=8] {'chord'}, use_global_device_ids=true, to_apply=%region_4.0 | all-reduce | flops 15360 | bytes 122880 | tf_op jit(solution)/shard_map/psum | solution.py:122
  234.9 18.2 %collective-permute-start.1 = (f32[3,1024]{0,1:T(8,128)S(1)}, f32[3,1024]{0,1:T(8,128)}, u32[]{:S(2)}, u32[]{:S(2)}) collective-permute-start(f32[3,1024]{0,1:T(8,128)S(1)} %get-tuple-element.61), channel_id=1, source_target_pairs={{8,0},{16,8},{24,16},{32,24},{40,32},{48,40},{56,48},{64,56},{72,6... | collective-permute-start | bytes 36872 | tf_op jit(solution)/shard_map/ppermute | solution.py:14
  257.1 8.7 %collective-permute-start.4 = (f32[6,64]{1,0:T(8,128)S(1)}, f32[6,64]{1,0:T(8,128)S(1)}, u32[]{:S(2)}, u32[]{:S(2)}) collective-permute-start(f32[6,64]{1,0:T(8,128)S(1)} %slice.401), channel_id=1, source_target_pairs={{8,0},{16,8},{24,16},{32,24},{40,32},{48,40},{56,48},{64,56},{72,6... | collective-permute-start | bytes 4616 | tf_op jit(solution)/shard_map/ppermute | solution.py:14
  280.1 68.6 %psum.30 = f32[6,1024]{0,1:T(8,128)S(1)} all-reduce(f32[6,1024]{0,1:T(8,128)} %fusion.85), channel_id=1, replica_groups=mesh['span'=64,'chord'=8] {'chord'}, use_global_device_ids=true, to_apply=%region_6.0 | all-reduce | flops 6144 | bytes 49152 | tf_op jit(solution)/shard_map/psum | solution.py:122
  350.9 19.7 %collective-permute-start.6 = (f32[6,64]{1,0:T(8,128)S(1)}, f32[6,64]{1,0:T(8,128)S(1)}, u32[]{:S(2)}, u32[]{:S(2)}) collective-permute-start(f32[6,64]{1,0:T(8,128)S(1)} %slice.405), channel_id=1, source_target_pairs={{8,0},{16,8},{24,16},{32,24},{40,32},{48,40},{56,48},{64,56},{72,6... | collective-permute-start | bytes 4616 | tf_op jit(solution)/shard_map/ppermute | solution.py:14
  380.8 78.4 %psum.31 = f32[6,1024]{0,1:T(8,128)S(1)} all-reduce(f32[6,1024]{0,1:T(8,128)S(1)} %fusion.86), channel_id=1, replica_groups=mesh['span'=64,'chord'=8] {'chord'}, use_global_device_ids=true, to_apply=%region_8.0 | all-reduce | flops 6144 | bytes 49152 | tf_op jit(solution)/shard_map/psum | solution.py:122
  460.2 13.6 %collective-permute-start.8 = (f32[3,1024]{1,0:T(4,128)S(1)}, f32[3,1024]{1,0:T(4,128)S(1)}, u32[]{:S(2)}, u32[]{:S(2)}) collective-permute-start(f32[3,1024]{1,0:T(4,128)S(1)} %slice.409), channel_id=1, source_target_pairs={{0,8},{8,16},{16,24},{24,32},{32,40},{40,48},{48,56},{56,64},{64,7... | collective-permute-start | bytes 36872 | tf_op jit(solution)/shard_map/ppermute | solution.py:25
  477.0 4.0 collective-permute-done.9
  481.5 4.0 gather_fusion.3
  489.5 14.8 %collective-permute-start.13 = (f32[5,16,10,1]{1,3,2,0:T(1,128)S(1)}, f32[5,16,10,1]{1,3,2,0:T(1,128)S(1)}, u32[]{:S(2)}, u32[]{:S(2)}) collective-permute-start(f32[5,16,10,1]{1,3,2,0:T(1,128)S(1)} %copy.116), channel_id=1, source_target_pairs={{0,1},{1,2},{2,3},{3,4},{4,5},{5,6},{6,7},{8,9},{9,10},{10,11},{11... | collective-permute-start | bytes 9608 | tf_op jit(solution)/shard_map/ppermute | solution.py:25
  510.7 9.3 %collective-permute-done.12 = f32[5,16,10,1]{1,3,2,0:T(1,128)S(1)} collective-permute-done((f32[5,16,10,1]{1,3,2,0:T(1,128)S(1)}, f32[5,16,10,1]{1,3,2,0:T(1,128)S(1)}, u32[]{:S(2)}, u32[]{:S(2)}) %collective-permute-start.12) | collective-permute-done | bytes 3232 | tf_op jit(solution)/shard_map/ppermute | solution.py:27
  524.7 3.5 collective-permute-start.15
  530.8 5.1 collective-permute-done.14
  536.9 3.9 collective-permute-start.17
  547.2 10.3 %collective-permute-done.16 = f32[5,16,10,1]{1,3,2,0:T(1,128)} collective-permute-done((f32[5,16,10,1]{1,3,2,0:T(1,128)}, f32[5,16,10,1]{1,3,2,0:T(1,128)}, u32[]{:S(2)}, u32[]{:S(2)}) %collective-permute-start.16) | collective-permute-done | bytes 3232 | tf_op jit(solution)/shard_map/ppermute | solution.py:27
  561.7 3.3 collective-permute-start.19
  567.5 5.2 collective-permute-done.18
  583.0 10.8 %collective-permute-done.20 = f32[5,16,10,1]{1,3,2,0:T(1,128)} collective-permute-done((f32[5,16,10,1]{1,3,2,0:T(1,128)}, f32[5,16,10,1]{1,3,2,0:T(1,128)}, u32[]{:S(2)}, u32[]{:S(2)}) %collective-permute-start.20) | collective-permute-done | bytes 3232 | tf_op jit(solution)/shard_map/ppermute | solution.py:27
  603.9 5.4 collective-permute-done.22
  613.6 3.6 collective-permute-start.24
  618.9 10.4 %collective-permute-done.24 = f32[5,16,10,1]{1,3,2,0:T(1,128)} collective-permute-done((f32[5,16,10,1]{1,3,2,0:T(1,128)}, f32[5,16,10,1]{1,3,2,0:T(1,128)}, u32[]{:S(2)}, u32[]{:S(2)}) %collective-permute-start.24) | collective-permute-done | bytes 3232 | tf_op jit(solution)/shard_map/ppermute | solution.py:27
  (253 shorter events, 117.9 us)
Async XLA Ops:
  1.4 16.0 %collective-permute-start.2 = (f32[6,64]{1,0:T(8,128)S(1)}, f32[6,64]{1,0:T(8,128)S(1)}, u32[]{:S(2)}, u32[]{:S(2)}) collective-permute-start(f32[6,64]{1,0:T(8,128)S(1)} %slice.324), channel_id=1, source_target_pairs={{8,0},{16,8},{24,16},{32,24},{40,32},{48,40},{56,48},{64,56},{72,6... | collective-permute-start | bytes 4616 | tf_op jit(solution)/shard_map/ppermute | solution.py:14
  5.8 481.1 %collective-permute-start.11 = (f32[5,16,1,128]{3,0,2,1:T(8,128)}, f32[5,16,1,128]{3,0,2,1:T(8,128)}, u32[]{:S(2)}, u32[]{:S(2)}) collective-permute-start(f32[5,16,1,128]{3,0,2,1:T(8,128)} %get-tuple-element.77), channel_id=1, source_target_pairs={{0,8},{8,16},{16,24},{24,32},{32,40},{40,48},{48,56},{56,64},{64,7... | collective-permute-start | bytes 122888 | tf_op jit(solution)/shard_map/ppermute | solution.py:25
  10.9 477.1 %collective-permute-start.10 = (f32[5,16,1,128]{3,0,2,1:T(8,128)}, f32[5,16,1,128]{3,0,2,1:T(8,128)}, u32[]{:S(2)}, u32[]{:S(2)}) collective-permute-start(f32[5,16,1,128]{3,0,2,1:T(8,128)} %get-tuple-element.76), channel_id=1, source_target_pairs={{8,0},{16,8},{24,16},{32,24},{40,32},{48,40},{56,48},{64,56},{72,6... | collective-permute-start | bytes 122888 | tf_op jit(solution)/shard_map/ppermute | solution.py:27
  22.8 13.2 %collective-permute-start.3 = (f32[6,64]{0,1:T(8,128)}, f32[6,64]{0,1:T(8,128)S(1)}, u32[]{:S(2)}, u32[]{:S(2)}) collective-permute-start(f32[6,64]{0,1:T(8,128)} %slice.400), channel_id=1, source_target_pairs={{0,8},{8,16},{16,24},{24,32},{32,40},{40,48},{48,56},{56,64},{64,7... | collective-permute-start | bytes 4616 | tf_op jit(solution)/shard_map/ppermute | solution.py:14
  233.0 21.0 %collective-permute-start = (f32[3,1024]{0,1:T(8,128)}, f32[3,1024]{0,1:T(8,128)S(1)}, u32[]{:S(2)}, u32[]{:S(2)}) collective-permute-start(f32[3,1024]{0,1:T(8,128)} %get-tuple-element.60), channel_id=1, source_target_pairs={{0,8},{8,16},{16,24},{24,32},{32,40},{40,48},{48,56},{56,64},{64,7... | collective-permute-start | bytes 36872 | tf_op jit(solution)/shard_map/ppermute | solution.py:14
  234.9 19.8 %collective-permute-start.1 = (f32[3,1024]{0,1:T(8,128)S(1)}, f32[3,1024]{0,1:T(8,128)}, u32[]{:S(2)}, u32[]{:S(2)}) collective-permute-start(f32[3,1024]{0,1:T(8,128)S(1)} %get-tuple-element.61), channel_id=1, source_target_pairs={{8,0},{16,8},{24,16},{32,24},{40,32},{48,40},{56,48},{64,56},{72,6... | collective-permute-start | bytes 36872 | tf_op jit(solution)/shard_map/ppermute | solution.py:14
  257.1 10.3 %collective-permute-start.4 = (f32[6,64]{1,0:T(8,128)S(1)}, f32[6,64]{1,0:T(8,128)S(1)}, u32[]{:S(2)}, u32[]{:S(2)}) collective-permute-start(f32[6,64]{1,0:T(8,128)S(1)} %slice.401), channel_id=1, source_target_pairs={{8,0},{16,8},{24,16},{32,24},{40,32},{48,40},{56,48},{64,56},{72,6... | collective-permute-start | bytes 4616 | tf_op jit(solution)/shard_map/ppermute | solution.py:14
  350.9 22.0 %collective-permute-start.6 = (f32[6,64]{1,0:T(8,128)S(1)}, f32[6,64]{1,0:T(8,128)S(1)}, u32[]{:S(2)}, u32[]{:S(2)}) collective-permute-start(f32[6,64]{1,0:T(8,128)S(1)} %slice.405), channel_id=1, source_target_pairs={{8,0},{16,8},{24,16},{32,24},{40,32},{48,40},{56,48},{64,56},{72,6... | collective-permute-start | bytes 4616 | tf_op jit(solution)/shard_map/ppermute | solution.py:14
  460.2 16.8 %collective-permute-start.8 = (f32[3,1024]{1,0:T(4,128)S(1)}, f32[3,1024]{1,0:T(4,128)S(1)}, u32[]{:S(2)}, u32[]{:S(2)}) collective-permute-start(f32[3,1024]{1,0:T(4,128)S(1)} %slice.409), channel_id=1, source_target_pairs={{0,8},{8,16},{16,24},{24,32},{32,40},{40,48},{48,56},{56,64},{64,7... | collective-permute-start | bytes 36872 | tf_op jit(solution)/shard_map/ppermute | solution.py:25
  473.8 7.2 %collective-permute-start.9 = (f32[3,1024]{1,0:T(4,128)S(1)}, f32[3,1024]{1,0:T(4,128)S(1)}, u32[]{:S(2)}, u32[]{:S(2)}) collective-permute-start(f32[3,1024]{1,0:T(4,128)S(1)} %slice.409), channel_id=1, source_target_pairs={{8,0},{16,8},{24,16},{32,24},{40,32},{48,40},{56,48},{64,56},{72,6... | collective-permute-start | bytes 36872 | tf_op jit(solution)/shard_map/ppermute | solution.py:27
  489.5 19.3 %collective-permute-start.13 = (f32[5,16,10,1]{1,3,2,0:T(1,128)S(1)}, f32[5,16,10,1]{1,3,2,0:T(1,128)S(1)}, u32[]{:S(2)}, u32[]{:S(2)}) collective-permute-start(f32[5,16,10,1]{1,3,2,0:T(1,128)S(1)} %copy.116), channel_id=1, source_target_pairs={{0,1},{1,2},{2,3},{3,4},{4,5},{5,6},{6,7},{8,9},{9,10},{10,11},{11... | collective-permute-start | bytes 9608 | tf_op jit(solution)/shard_map/ppermute | solution.py:25
  504.6 15.4 %collective-permute-start.12 = (f32[5,16,10,1]{1,3,2,0:T(1,128)S(1)}, f32[5,16,10,1]{1,3,2,0:T(1,128)S(1)}, u32[]{:S(2)}, u32[]{:S(2)}) collective-permute-start(f32[5,16,10,1]{1,3,2,0:T(1,128)S(1)} %copy.113), channel_id=1, source_target_pairs={{1,0},{2,1},{3,2},{4,3},{5,4},{6,5},{7,6},{9,8},{10,9},{11,10},{12... | collective-permute-start | bytes 9608 | tf_op jit(solution)/shard_map/ppermute | solution.py:27
  524.7 6.0 collective-permute-start.15
  528.2 7.7 %collective-permute-start.14 = (f32[5,16,1,128]{3,0,2,1:T(8,128)S(1)}, f32[5,16,1,128]{3,0,2,1:T(8,128)S(1)}, u32[]{:S(2)}, u32[]{:S(2)}) collective-permute-start(f32[5,16,1,128]{3,0,2,1:T(8,128)S(1)} %get-tuple-element.75), channel_id=1, source_target_pairs={{8,0},{16,8},{24,16},{32,24},{40,32},{48,40},{56,48},{64,56},{72,6... | collective-permute-start | bytes 122888 | tf_op jit(solution)/shard_map/ppermute | solution.py:27
  536.9 7.6 %collective-permute-start.17 = (f32[5,16,10,1]{1,3,2,0:T(1,128)S(1)}, f32[5,16,10,1]{1,3,2,0:T(1,128)}, u32[]{:S(2)}, u32[]{:S(2)}) collective-permute-start(f32[5,16,10,1]{1,3,2,0:T(1,128)S(1)} %copy.121), channel_id=1, source_target_pairs={{0,1},{1,2},{2,3},{3,4},{4,5},{5,6},{6,7},{8,9},{9,10},{10,11},{11... | collective-permute-start | bytes 9608 | tf_op jit(solution)/shard_map/ppermute | solution.py:25
  541.8 15.7 %collective-permute-start.16 = (f32[5,16,10,1]{1,3,2,0:T(1,128)}, f32[5,16,10,1]{1,3,2,0:T(1,128)}, u32[]{:S(2)}, u32[]{:S(2)}) collective-permute-start(f32[5,16,10,1]{1,3,2,0:T(1,128)} %copy.119), channel_id=1, source_target_pairs={{1,0},{2,1},{3,2},{4,3},{5,4},{6,5},{7,6},{9,8},{10,9},{11,10},{12... | collective-permute-start | bytes 9608 | tf_op jit(solution)/shard_map/ppermute | solution.py:27
  561.7 5.8 collective-permute-start.19
  565.0 7.7 %collective-permute-start.18 = (f32[5,16,1,128]{3,0,2,1:T(8,128)S(1)}, f32[5,16,1,128]{3,0,2,1:T(8,128)S(1)}, u32[]{:S(2)}, u32[]{:S(2)}) collective-permute-start(f32[5,16,1,128]{3,0,2,1:T(8,128)S(1)} %get-tuple-element.73), channel_id=1, source_target_pairs={{8,0},{16,8},{24,16},{32,24},{40,32},{48,40},{56,48},{64,56},{72,6... | collective-permute-start | bytes 122888 | tf_op jit(solution)/shard_map/ppermute | solution.py:27
  574.0 7.0 %collective-permute-start.21 = (f32[5,16,10,1]{1,3,2,0:T(1,128)S(1)}, f32[5,16,10,1]{1,3,2,0:T(1,128)S(1)}, u32[]{:S(2)}, u32[]{:S(2)}) collective-permute-start(f32[5,16,10,1]{1,3,2,0:T(1,128)S(1)} %copy.125), channel_id=1, source_target_pairs={{0,1},{1,2},{2,3},{3,4},{4,5},{5,6},{6,7},{8,9},{9,10},{10,11},{11... | collective-permute-start | bytes 9608 | tf_op jit(solution)/shard_map/ppermute | solution.py:25
  578.1 15.7 %collective-permute-start.20 = (f32[5,16,10,1]{1,3,2,0:T(1,128)}, f32[5,16,10,1]{1,3,2,0:T(1,128)}, u32[]{:S(2)}, u32[]{:S(2)}) collective-permute-start(f32[5,16,10,1]{1,3,2,0:T(1,128)} %copy.123), channel_id=1, source_target_pairs={{1,0},{2,1},{3,2},{4,3},{5,4},{6,5},{7,6},{9,8},{10,9},{11,10},{12... | collective-permute-start | bytes 9608 | tf_op jit(solution)/shard_map/ppermute | solution.py:27
  598.1 5.9 collective-permute-start.23
  601.4 8.0 %collective-permute-start.22 = (f32[5,16,1,128]{3,0,2,1:T(8,128)S(1)}, f32[5,16,1,128]{3,0,2,1:T(8,128)S(1)}, u32[]{:S(2)}, u32[]{:S(2)}) collective-permute-start(f32[5,16,1,128]{3,0,2,1:T(8,128)S(1)} %get-tuple-element.71), channel_id=1, source_target_pairs={{8,0},{16,8},{24,16},{32,24},{40,32},{48,40},{56,48},{64,56},{72,6... | collective-permute-start | bytes 122888 | tf_op jit(solution)/shard_map/ppermute | solution.py:27
  610.7 7.1 %collective-permute-start.25 = (f32[5,16,10,1]{1,3,2,0:T(1,128)S(1)}, f32[5,16,10,1]{1,3,2,0:T(1,128)S(1)}, u32[]{:S(2)}, u32[]{:S(2)}) collective-permute-start(f32[5,16,10,1]{1,3,2,0:T(1,128)S(1)} %copy.129), channel_id=1, source_target_pairs={{0,1},{1,2},{2,3},{3,4},{4,5},{5,6},{6,7},{8,9},{9,10},{10,11},{11... | collective-permute-start | bytes 9608 | tf_op jit(solution)/shard_map/ppermute | solution.py:25
  613.6 15.7 %collective-permute-start.24 = (f32[5,16,10,1]{1,3,2,0:T(1,128)}, f32[5,16,10,1]{1,3,2,0:T(1,128)}, u32[]{:S(2)}, u32[]{:S(2)}) collective-permute-start(f32[5,16,10,1]{1,3,2,0:T(1,128)} %copy.127), channel_id=1, source_target_pairs={{1,0},{2,1},{3,2},{4,3},{5,4},{6,5},{7,6},{9,8},{10,9},{11,10},{12... | collective-permute-start | bytes 9608 | tf_op jit(solution)/shard_map/ppermute | solution.py:27
  (45 other events, 463.7 us)
where the time goes:
time: 643 us; the launch traced here: 633 us
  blocking collectives  341 us (53%)
  starting transfers between devices  132 us (21%)
  waiting for transfers between devices  62.9 us (10%)
  local copies, waits for them, and re-layouts  44.4 us (7%)
  matrix products  26.3 us (4%)
  other arithmetic  22.7 us (4%)
    psum x3, blocking collectives, per_device(): stiff_total = lax.psum(local_forces, 'chord')  341 us
    ppermute x9, waiting for transfers between devices, with_halo(): lax.ppermute(head, axis, [((i + 1) % count, i) for i in range(ends)])  60.6 us
    ppermute x8, starting transfers between devices, shifted(): lax.ppermute(value, axis, [(source, source + steps) for source in range(i...  60.6 us
    ppermute x9, starting transfers between devices, with_halo(): lax.ppermute(tail, axis, [(i, (i + 1) % count) for i in range(ends)])  52.4 us
    ppermute x9, starting transfers between devices, with_halo(): lax.ppermute(head, axis, [((i + 1) % count, i) for i in range(ends)])  19.4 us
    dot_general x12, matrix products, relax_cells(): jnp.einsum('ij,jnsc->insc', downwind[direction], backward, precision=lax....  13.2 us
  transfers between devices with their start and end apart: 26, of which 11 were waited for; matrix products, arithmetic and copies ran while one was open for 11% of the time, Pallas kernels for 0%

commit v1 on v0

--- a/solution.py
+++ b/solution.py
@@ -119,7 +119,7 @@
     shell_state = adjoint_shell
     for turn_index in range(SS):
         local_forces = element_terms(shell_state, element_stiffness, local_nodes)
-        stiff_total = lax.psum(local_forces, "chord")
+        stiff_total = jnp.sum(lax.all_gather(local_forces, axis_name="chord"), axis=0)
         residual = shell_grad - load_full - stiff_total
         shell_state = shell_state + jnp.einsum(
             "ijn,jn->in", node_precond, residual, precision=lax.Precision.HIGHEST

time: 643 us -> 510 us (0.79)
  the two profiles are of different devices: /device:TPU:223 before, /device:TPU:152 now
where the time goes in v1:
time: 510 us; the launch traced here: 500 us
  blocking collectives  257 us (50%)
  waiting for transfers between devices  87.5 us (17%)
  starting transfers between devices  79.9 us (16%)
  matrix products  28.3 us (6%)
  local copies, waits for them, and re-layouts  25.5 us (5%)
  other arithmetic  19.6 us (4%)
    all_gather x3, blocking collectives, per_device(): lax.all_gather(local_forces, axis_name='chord')  191 us
    psum x1, blocking collectives, per_device(): partial_value = lax.psum(partial_value, 'chord')  65.9 us
    ppermute x9, waiting for transfers between devices, with_halo(): lax.ppermute(head, axis, [((i + 1) % count, i) for i in range(ends)])  44.1 us
    ppermute x9, starting transfers between devices, with_halo(): lax.ppermute(tail, axis, [(i, (i + 1) % count) for i in range(ends)])  36.1 us
    ppermute x9, starting transfers between devices, with_halo(): lax.ppermute(head, axis, [((i + 1) % count, i) for i in range(ends)])  25.2 us
    ppermute x9, waiting for transfers between devices, with_halo(): lax.ppermute(tail, axis, [(i, (i + 1) % count) for i in range(ends)])  23.3 us
    ppermute x8, waiting for transfers between devices, shifted(): lax.ppermute(value, axis, [(source, source + steps) for source in range(i...  20.1 us
    ppermute x8, starting transfers between devices, shifted(): lax.ppermute(value, axis, [(source, source + steps) for source in range(i...  18.6 us
  transfers between devices with their start and end apart: 26, of which 12 were waited for; matrix products, arithmetic and copies ran while one was open for 11% of the time, Pallas kernels for 0%

profile of v1, /device:TPU:152, one launch (start us, length us, event | category | flops | bytes accessed | tf_op | source)
XLA Modules:
  0.0 500.1 jit_solution(6169982924030445527)
XLA Ops:
  1.3 3.6 collective-permute-start.2
  8.9 6.4 %scatter_custom_fusion = f32[3072,3]{1,0:T(8,128)S(1)} fusion(s32[1024]{0:T(1024)S(1)} %subtract_bitcast_fusion.3, f32[1024,3]{1,0:T(8,128)S(1)} %bitcast.209, f32[]{:T(128)} %constant.118.clone.1), kind=kCustom, calls=%fused_computation.52 | custom fusion | flops 3072 | bytes 36868 | tf_op jit(solution)/shard_map/scatter-add | solution.py:112
  15.8 65.9 %psum.7 = f32[3,3072]{1,0:T(4,128)S(1)} all-reduce(f32[3,3072]{1,0:T(4,128)S(1)} %bitcast.213), channel_id=1, replica_groups=mesh['span'=64,'chord'=8] {'chord'}, use_global_device_ids=true, to_apply=%region_1.0 | all-reduce | flops 9216 | bytes 73728 | tf_op jit(solution)/shard_map/psum | solution.py:115
  89.5 7.0 %collective-permute-start.10 = (f32[5,16,1,128]{3,0,2,1:T(8,128)}, f32[5,16,1,128]{3,0,2,1:T(8,128)}, u32[]{:S(2)}, u32[]{:S(2)}) collective-permute-start(f32[5,16,1,128]{3,0,2,1:T(8,128)} %get-tuple-element.76), channel_id=1, source_target_pairs={{8,0},{16,8},{24,16},{32,24},{40,32},{48,40},{56,48},{64,56},{72,6... | collective-permute-start | bytes 122888 | tf_op jit(solution)/shard_map/ppermute | solution.py:27
  104.6 6.6 %collective-permute-done.3 = f32[6,64]{0,1:T(8,128)S(1)} collective-permute-done((f32[6,64]{0,1:T(8,128)S(1)}, f32[6,64]{0,1:T(8,128)S(1)}, u32[]{:S(2)}, u32[]{:S(2)}) %collective-permute-start.3) | collective-permute-done | bytes 1568 | tf_op jit(solution)/shard_map/ppermute | solution.py:14
  112.0 63.6 %all_gather.26 = f32[8,6,1024]{2,1,0:T(8,128)S(1)} all-gather(f32[1,6,1024]{2,1,0:T(8,128)S(1)} %copy.190), channel_id=1, replica_groups=mesh['span'=64,'chord'=8] {'chord'}, dimensions={0}, use_global_device_ids=true | all-gather | bytes 221184 | tf_op jit(solution)/shard_map/all_gather | solution.py:122
  187.3 6.1 %collective-permute-done.5 = f32[6,64]{0,1:T(8,128)S(1)} collective-permute-done((f32[6,64]{0,1:T(8,128)S(1)}, f32[6,64]{0,1:T(8,128)S(1)}, u32[]{:S(2)}, u32[]{:S(2)}) %collective-permute-start.5) | collective-permute-done | bytes 1568 | tf_op jit(solution)/shard_map/ppermute | solution.py:14
  194.3 63.3 %all_gather.29 = f32[8,6,1024]{2,1,0:T(8,128)S(1)} all-gather(f32[1,6,1024]{2,1,0:T(8,128)S(1)} %copy.194), channel_id=1, replica_groups=mesh['span'=64,'chord'=8] {'chord'}, dimensions={0}, use_global_device_ids=true | all-gather | bytes 221184 | tf_op jit(solution)/shard_map/all_gather | solution.py:122
  267.3 6.6 %collective-permute-done.7 = f32[6,64]{0,1:T(8,128)S(1)} collective-permute-done((f32[6,64]{0,1:T(8,128)S(1)}, f32[6,64]{0,1:T(8,128)S(1)}, u32[]{:S(2)}, u32[]{:S(2)}) %collective-permute-start.7) | collective-permute-done | bytes 1568 | tf_op jit(solution)/shard_map/ppermute | solution.py:14
  274.7 63.7 %all_gather.32 = f32[8,6,1024]{2,1,0:T(8,128)S(1)} all-gather(f32[1,6,1024]{2,1,0:T(8,128)S(1)} %copy.198), channel_id=1, replica_groups=mesh['span'=64,'chord'=8] {'chord'}, dimensions={0}, use_global_device_ids=true | all-gather | bytes 221184 | tf_op jit(solution)/shard_map/all_gather | solution.py:122
  343.2 5.7 %collective-permute-done.8 = f32[3,1024]{1,0:T(4,128)S(1)} collective-permute-done((f32[3,1024]{1,0:T(4,128)S(1)}, f32[3,1024]{1,0:T(4,128)S(1)}, u32[]{:S(2)}, u32[]{:S(2)}) %collective-permute-start.8) | collective-permute-done | bytes 12320 | tf_op jit(solution)/shard_map/ppermute | solution.py:25
  349.4 4.0 gather_fusion.3
  357.3 15.0 %collective-permute-start.13 = (f32[5,16,10,1]{1,3,2,0:T(1,128)S(1)}, f32[5,16,10,1]{1,3,2,0:T(1,128)S(1)}, u32[]{:S(2)}, u32[]{:S(2)}) collective-permute-start(f32[5,16,10,1]{1,3,2,0:T(1,128)S(1)} %copy.214), channel_id=1, source_target_pairs={{0,1},{1,2},{2,3},{3,4},{4,5},{5,6},{6,7},{8,9},{9,10},{10,11},{11... | collective-permute-start | bytes 9608 | tf_op jit(solution)/shard_map/ppermute | solution.py:25
  378.7 10.5 %collective-permute-done.12 = f32[5,16,10,1]{1,3,2,0:T(1,128)S(1)} collective-permute-done((f32[5,16,10,1]{1,3,2,0:T(1,128)S(1)}, f32[5,16,10,1]{1,3,2,0:T(1,128)S(1)}, u32[]{:S(2)}, u32[]{:S(2)}) %collective-permute-start.12) | collective-permute-done | bytes 3232 | tf_op jit(solution)/shard_map/ppermute | solution.py:27
  398.9 5.9 %collective-permute-done.15 = f32[5,16,1,128]{3,0,2,1:T(8,128)S(1)} collective-permute-done((f32[5,16,1,128]{3,0,2,1:T(8,128)S(1)}, f32[5,16,1,128]{3,0,2,1:T(8,128)S(1)}, u32[]{:S(2)}, u32[]{:S(2)}) %collective-permute-start.15) | collective-permute-done | bytes 40992 | tf_op jit(solution)/shard_map/ppermute | solution.py:25
  405.5 4.3 collective-permute-start.17
  414.7 12.0 %collective-permute-done.16 = f32[5,16,10,1]{1,3,2,0:T(1,128)S(1)} collective-permute-done((f32[5,16,10,1]{1,3,2,0:T(1,128)S(1)}, f32[5,16,10,1]{1,3,2,0:T(1,128)S(1)}, u32[]{:S(2)}, u32[]{:S(2)}) %collective-permute-start.16) | collective-permute-done | bytes 3232 | tf_op jit(solution)/shard_map/ppermute | solution.py:27
  435.2 5.9 %collective-permute-done.19 = f32[5,16,1,128]{3,0,2,1:T(8,128)S(1)} collective-permute-done((f32[5,16,1,128]{3,0,2,1:T(8,128)S(1)}, f32[5,16,1,128]{3,0,2,1:T(8,128)S(1)}, u32[]{:S(2)}, u32[]{:S(2)}) %collective-permute-start.19) | collective-permute-done | bytes 40992 | tf_op jit(solution)/shard_map/ppermute | solution.py:25
  441.8 2.8 collective-permute-start.21
  444.9 3.1 collective-permute-start.20
  450.5 11.0 %collective-permute-done.20 = f32[5,16,10,1]{1,3,2,0:T(1,128)S(1)} collective-permute-done((f32[5,16,10,1]{1,3,2,0:T(1,128)S(1)}, f32[5,16,10,1]{1,3,2,0:T(1,128)S(1)}, u32[]{:S(2)}, u32[]{:S(2)}) %collective-permute-start.20) | collective-permute-done | bytes 3232 | tf_op jit(solution)/shard_map/ppermute | solution.py:27
  470.0 5.9 %collective-permute-done.23 = f32[5,16,1,128]{3,0,2,1:T(8,128)S(1)} collective-permute-done((f32[5,16,1,128]{3,0,2,1:T(8,128)S(1)}, f32[5,16,1,128]{3,0,2,1:T(8,128)S(1)}, u32[]{:S(2)}, u32[]{:S(2)}) %collective-permute-start.23) | collective-permute-done | bytes 40992 | tf_op jit(solution)/shard_map/ppermute | solution.py:25
  479.5 3.5 collective-permute-start.24
  485.5 10.6 %collective-permute-done.24 = f32[5,16,10,1]{1,3,2,0:T(1,128)S(1)} collective-permute-done((f32[5,16,10,1]{1,3,2,0:T(1,128)S(1)}, f32[5,16,10,1]{1,3,2,0:T(1,128)S(1)}, u32[]{:S(2)}, u32[]{:S(2)}) %collective-permute-start.24) | collective-permute-done | bytes 3232 | tf_op jit(solution)/shard_map/ppermute | solution.py:27
  (223 shorter events, 104.6 us)
Async XLA Ops:
  1.3 97.2 %collective-permute-start.2 = (f32[6,64]{1,0:T(8,128)S(1)}, f32[6,64]{1,0:T(8,128)S(1)}, u32[]{:S(2)}, u32[]{:S(2)}) collective-permute-start(f32[6,64]{1,0:T(8,128)S(1)} %slice.324), channel_id=1, source_target_pairs={{8,0},{16,8},{24,16},{32,24},{40,32},{48,40},{56,48},{64,56},{72,6... | collective-permute-start | bytes 4616 | tf_op jit(solution)/shard_map/ppermute | solution.py:14
  82.3 93.3 %collective-permute-start.1 = (f32[3,1024]{1,0:T(4,128)}, f32[3,1024]{1,0:T(4,128)}, u32[]{:S(2)}, u32[]{:S(2)}) collective-permute-start(f32[3,1024]{1,0:T(4,128)} %get-tuple-element.82), channel_id=1, source_target_pairs={{8,0},{16,8},{24,16},{32,24},{40,32},{48,40},{56,48},{64,56},{72,6... | collective-permute-start | bytes 36872 | tf_op jit(solution)/shard_map/ppermute | solution.py:14
  84.2 91.4 %collective-permute-start = (f32[3,1024]{1,0:T(4,128)}, f32[3,1024]{1,0:T(4,128)}, u32[]{:S(2)}, u32[]{:S(2)}) collective-permute-start(f32[3,1024]{1,0:T(4,128)} %get-tuple-element.81), channel_id=1, source_target_pairs={{0,8},{8,16},{16,24},{24,32},{32,40},{40,48},{48,56},{56,64},{64,7... | collective-permute-start | bytes 36872 | tf_op jit(solution)/shard_map/ppermute | solution.py:14
  87.5 267.3 %collective-permute-start.11 = (f32[5,16,1,128]{3,0,2,1:T(8,128)}, f32[5,16,1,128]{3,0,2,1:T(8,128)}, u32[]{:S(2)}, u32[]{:S(2)}) collective-permute-start(f32[5,16,1,128]{3,0,2,1:T(8,128)} %get-tuple-element.77), channel_id=1, source_target_pairs={{0,8},{8,16},{16,24},{24,32},{32,40},{40,48},{48,56},{56,64},{64,7... | collective-permute-start | bytes 122888 | tf_op jit(solution)/shard_map/ppermute | solution.py:25
  89.5 266.4 %collective-permute-start.10 = (f32[5,16,1,128]{3,0,2,1:T(8,128)}, f32[5,16,1,128]{3,0,2,1:T(8,128)}, u32[]{:S(2)}, u32[]{:S(2)}) collective-permute-start(f32[5,16,1,128]{3,0,2,1:T(8,128)} %get-tuple-element.76), channel_id=1, source_target_pairs={{8,0},{16,8},{24,16},{32,24},{40,32},{48,40},{56,48},{64,56},{72,6... | collective-permute-start | bytes 122888 | tf_op jit(solution)/shard_map/ppermute | solution.py:27
  102.6 8.6 %collective-permute-start.3 = (f32[6,64]{0,1:T(8,128)S(1)}, f32[6,64]{0,1:T(8,128)S(1)}, u32[]{:S(2)}, u32[]{:S(2)}) collective-permute-start(f32[6,64]{0,1:T(8,128)S(1)} %slice.400), channel_id=1, source_target_pairs={{0,8},{8,16},{16,24},{24,32},{32,40},{40,48},{48,56},{56,64},{64,7... | collective-permute-start | bytes 4616 | tf_op jit(solution)/shard_map/ppermute | solution.py:14
  184.9 8.6 %collective-permute-start.5 = (f32[6,64]{0,1:T(8,128)S(1)}, f32[6,64]{0,1:T(8,128)S(1)}, u32[]{:S(2)}, u32[]{:S(2)}) collective-permute-start(f32[6,64]{0,1:T(8,128)S(1)} %slice.404), channel_id=1, source_target_pairs={{0,8},{8,16},{16,24},{24,32},{32,40},{40,48},{48,56},{56,64},{64,7... | collective-permute-start | bytes 4616 | tf_op jit(solution)/shard_map/ppermute | solution.py:14
  265.2 8.7 %collective-permute-start.7 = (f32[6,64]{0,1:T(8,128)S(1)}, f32[6,64]{0,1:T(8,128)S(1)}, u32[]{:S(2)}, u32[]{:S(2)}) collective-permute-start(f32[6,64]{0,1:T(8,128)S(1)} %slice.408), channel_id=1, source_target_pairs={{0,8},{8,16},{16,24},{24,32},{32,40},{40,48},{48,56},{56,64},{64,7... | collective-permute-start | bytes 4616 | tf_op jit(solution)/shard_map/ppermute | solution.py:14
  338.5 4.6 collective-permute-start.9
  340.5 8.4 %collective-permute-start.8 = (f32[3,1024]{1,0:T(4,128)S(1)}, f32[3,1024]{1,0:T(4,128)S(1)}, u32[]{:S(2)}, u32[]{:S(2)}) collective-permute-start(f32[3,1024]{1,0:T(4,128)S(1)} %slice.409), channel_id=1, source_target_pairs={{0,8},{8,16},{16,24},{24,32},{32,40},{40,48},{48,56},{56,64},{64,7... | collective-permute-start | bytes 36872 | tf_op jit(solution)/shard_map/ppermute | solution.py:25
  357.3 19.5 %collective-permute-start.13 = (f32[5,16,10,1]{1,3,2,0:T(1,128)S(1)}, f32[5,16,10,1]{1,3,2,0:T(1,128)S(1)}, u32[]{:S(2)}, u32[]{:S(2)}) collective-permute-start(f32[5,16,10,1]{1,3,2,0:T(1,128)S(1)} %copy.214), channel_id=1, source_target_pairs={{0,1},{1,2},{2,3},{3,4},{4,5},{5,6},{6,7},{8,9},{9,10},{10,11},{11... | collective-permute-start | bytes 9608 | tf_op jit(solution)/shard_map/ppermute | solution.py:25
  372.7 16.5 %collective-permute-start.12 = (f32[5,16,10,1]{1,3,2,0:T(1,128)S(1)}, f32[5,16,10,1]{1,3,2,0:T(1,128)S(1)}, u32[]{:S(2)}, u32[]{:S(2)}) collective-permute-start(f32[5,16,10,1]{1,3,2,0:T(1,128)S(1)} %copy.211), channel_id=1, source_target_pairs={{1,0},{2,1},{3,2},{4,3},{5,4},{6,5},{7,6},{9,8},{10,9},{11,10},{12... | collective-permute-start | bytes 9608 | tf_op jit(solution)/shard_map/ppermute | solution.py:27
  394.0 5.0 collective-permute-start.14
  395.9 8.9 %collective-permute-start.15 = (f32[5,16,1,128]{3,0,2,1:T(8,128)S(1)}, f32[5,16,1,128]{3,0,2,1:T(8,128)S(1)}, u32[]{:S(2)}, u32[]{:S(2)}) collective-permute-start(f32[5,16,1,128]{3,0,2,1:T(8,128)S(1)} %get-tuple-element.74), channel_id=1, source_target_pairs={{0,8},{8,16},{16,24},{24,32},{32,40},{40,48},{48,56},{56,64},{64,7... | collective-permute-start | bytes 122888 | tf_op jit(solution)/shard_map/ppermute | solution.py:25
  405.5 8.1 %collective-permute-start.17 = (f32[5,16,10,1]{1,3,2,0:T(1,128)S(1)}, f32[5,16,10,1]{1,3,2,0:T(1,128)S(1)}, u32[]{:S(2)}, u32[]{:S(2)}) collective-permute-start(f32[5,16,10,1]{1,3,2,0:T(1,128)S(1)} %copy.219), channel_id=1, source_target_pairs={{0,1},{1,2},{2,3},{3,4},{4,5},{5,6},{6,7},{8,9},{9,10},{10,11},{11... | collective-permute-start | bytes 9608 | tf_op jit(solution)/shard_map/ppermute | solution.py:25
  410.1 16.5 %collective-permute-start.16 = (f32[5,16,10,1]{1,3,2,0:T(1,128)S(1)}, f32[5,16,10,1]{1,3,2,0:T(1,128)S(1)}, u32[]{:S(2)}, u32[]{:S(2)}) collective-permute-start(f32[5,16,10,1]{1,3,2,0:T(1,128)S(1)} %copy.217), channel_id=1, source_target_pairs={{1,0},{2,1},{3,2},{4,3},{5,4},{6,5},{7,6},{9,8},{10,9},{11,10},{12... | collective-permute-start | bytes 9608 | tf_op jit(solution)/shard_map/ppermute | solution.py:27
  430.2 4.9 collective-permute-start.18
  432.2 8.9 %collective-permute-start.19 = (f32[5,16,1,128]{3,0,2,1:T(8,128)S(1)}, f32[5,16,1,128]{3,0,2,1:T(8,128)S(1)}, u32[]{:S(2)}, u32[]{:S(2)}) collective-permute-start(f32[5,16,1,128]{3,0,2,1:T(8,128)S(1)} %get-tuple-element.72), channel_id=1, source_target_pairs={{0,8},{8,16},{16,24},{24,32},{32,40},{40,48},{48,56},{56,64},{64,7... | collective-permute-start | bytes 122888 | tf_op jit(solution)/shard_map/ppermute | solution.py:25
  441.8 7.6 %collective-permute-start.21 = (f32[5,16,10,1]{1,3,2,0:T(1,128)S(1)}, f32[5,16,10,1]{1,3,2,0:T(1,128)S(1)}, u32[]{:S(2)}, u32[]{:S(2)}) collective-permute-start(f32[5,16,10,1]{1,3,2,0:T(1,128)S(1)} %copy.223), channel_id=1, source_target_pairs={{0,1},{1,2},{2,3},{3,4},{4,5},{5,6},{6,7},{8,9},{9,10},{10,11},{11... | collective-permute-start | bytes 9608 | tf_op jit(solution)/shard_map/ppermute | solution.py:25
  444.9 16.5 %collective-permute-start.20 = (f32[5,16,10,1]{1,3,2,0:T(1,128)S(1)}, f32[5,16,10,1]{1,3,2,0:T(1,128)S(1)}, u32[]{:S(2)}, u32[]{:S(2)}) collective-permute-start(f32[5,16,10,1]{1,3,2,0:T(1,128)S(1)} %copy.221), channel_id=1, source_target_pairs={{1,0},{2,1},{3,2},{4,3},{5,4},{6,5},{7,6},{9,8},{10,9},{11,10},{12... | collective-permute-start | bytes 9608 | tf_op jit(solution)/shard_map/ppermute | solution.py:27
  465.0 4.9 collective-permute-start.22
  467.0 8.9 %collective-permute-start.23 = (f32[5,16,1,128]{3,0,2,1:T(8,128)S(1)}, f32[5,16,1,128]{3,0,2,1:T(8,128)S(1)}, u32[]{:S(2)}, u32[]{:S(2)}) collective-permute-start(f32[5,16,1,128]{3,0,2,1:T(8,128)S(1)} %get-tuple-element.70), channel_id=1, source_target_pairs={{0,8},{8,16},{16,24},{24,32},{32,40},{40,48},{48,56},{56,64},{64,7... | collective-permute-start | bytes 122888 | tf_op jit(solution)/shard_map/ppermute | solution.py:25
  476.5 7.8 %collective-permute-start.25 = (f32[5,16,10,1]{1,3,2,0:T(1,128)S(1)}, f32[5,16,10,1]{1,3,2,0:T(1,128)S(1)}, u32[]{:S(2)}, u32[]{:S(2)}) collective-permute-start(f32[5,16,10,1]{1,3,2,0:T(1,128)S(1)} %copy.227), channel_id=1, source_target_pairs={{0,1},{1,2},{2,3},{3,4},{4,5},{5,6},{6,7},{8,9},{9,10},{10,11},{11... | collective-permute-start | bytes 9608 | tf_op jit(solution)/shard_map/ppermute | solution.py:25
  479.5 16.5 %collective-permute-start.24 = (f32[5,16,10,1]{1,3,2,0:T(1,128)S(1)}, f32[5,16,10,1]{1,3,2,0:T(1,128)S(1)}, u32[]{:S(2)}, u32[]{:S(2)}) collective-permute-start(f32[5,16,10,1]{1,3,2,0:T(1,128)S(1)} %copy.225), channel_id=1, source_target_pairs={{1,0},{2,1},{3,2},{4,3},{5,4},{6,5},{7,6},{9,8},{10,9},{11,10},{12... | collective-permute-start | bytes 9608 | tf_op jit(solution)/shard_map/ppermute | solution.py:27
  (28 other events, 1135.9 us)
